TPU v7x, 32 devices: a whole 2x2x4 slice. The times are simulated.
32 devices in a mesh: tok: 2 (over x), head: 16 (over z, y, core).
Axes of the slice: x: 2, y: 2, z: 4, core: 2. Of those that a mesh axis runs over, the one named last changes fastest.
Arguments:
- query_states: bfloat16 [4096, 4096], P(('tok', 'head')), may hold values from -7.5 to 7.5
- key_states: bfloat16 [4096, 4096], P(('tok', 'head')), may hold values from -7.5 to 7.5
- value_states: bfloat16 [4096, 4096], P(('tok', 'head')), may hold values from -6 to 6
- token_rates: float32 [16, 4096], P('head', 'tok'), may hold values from 0.05 to 1
- fast_weights: bfloat16 [16, 512, 768], P('head'), may hold values from -0.375 to 0.375
Outputs:
- combined: bfloat16 [4096, 4096], P(('tok', 'head'))
- new_weights: bfloat16 [16, 512, 768], P('head', 'tok')
All inputs are finite; a program needn't handle non-finite values.
Results may differ from a plain program's by a relative error of at most 0.039.
Values may be sent and summed in bfloat16 or wider, within the bound.
A program may use at most 64 MiB of HBM per device.

v0:
```python
import jax
import jax.numpy as jnp
from jax import lax
from jax.sharding import PartitionSpec as P

DH = 256
FH = 512
WINDOW = 1024
NS_STEPS = 5


coef_linear = 3.4445
coef_cubic = -4.775
coef_quintic = 2.0315
epsilon = 1e-06


def shifted(value, axis, steps):
    count = lax.axis_size(axis)
    first, last = (max(0, -steps), min(count, count - steps))
    return lax.ppermute(value, axis, [(source, source + steps) for source in range(first, last)])


def block_size():
    return 512


def rms_norm(values):
    return values * lax.rsqrt(jnp.mean(values * values, axis=-1, keepdims=True) + epsilon)


def silu_parts(gate_value):
    sigmoid = jax.nn.sigmoid(gate_value)
    return (gate_value * sigmoid, sigmoid * (1.0 + gate_value * (1.0 - sigmoid)))


def across(inputs, weight_rows):
    return lax.dot_general(
        inputs, weight_rows, (((1,), (1,)), ((), ())), preferred_element_type=jnp.float32
    )


def apply_rows(query_rows, weight_rows):
    query_gate = across(query_rows, weight_rows[:, :DH])
    query_up = across(query_rows, weight_rows[:, DH : 2 * DH])
    query_hidden = (jax.nn.silu(query_gate) * query_up).astype(jnp.bfloat16)
    return jnp.dot(query_hidden, weight_rows[:, 2 * DH :], preferred_element_type=jnp.float32)


def attend(query_rows, key_rows, value_rows, positions, key_positions):
    scores = jnp.dot(query_rows, key_rows.T, preferred_element_type=jnp.float32) * DH ** (-0.5)
    offset = positions[:, None] - key_positions[None, :]
    allowed = (offset >= 0) & (offset < WINDOW) & (key_positions[None, :] >= 0)
    scores = jnp.where(allowed, scores, -1e30)
    highest = jnp.max(scores, axis=1, keepdims=True)
    expo = jnp.exp(scores - highest)
    probs = (expo / jnp.sum(expo, axis=1, keepdims=True)).astype(jnp.bfloat16)
    return jnp.dot(probs, value_rows, preferred_element_type=jnp.float32)


def polish(iterate, gram_matrix):
    square_gram = jnp.einsum(
        "jde,jef->jdf", gram_matrix, gram_matrix, preferred_element_type=jnp.float32
    )
    polynomial = (coef_cubic * gram_matrix.astype(jnp.float32) + coef_quintic * square_gram).astype(
        jnp.bfloat16
    )
    product = jnp.einsum("fjd,jde->fje", iterate, polynomial, preferred_element_type=jnp.float32)
    return (coef_linear * iterate.astype(jnp.float32) + product).astype(jnp.bfloat16)


def per_device(query_states, key_states, value_states, token_rates, fast_weights):
    query_rows, key_rows, value_rows = (
        lax.all_to_all(query_states, "head", split_axis=1, concat_axis=0, tiled=True),
        lax.all_to_all(key_states, "head", split_axis=1, concat_axis=0, tiled=True),
        lax.all_to_all(value_states, "head", split_axis=1, concat_axis=0, tiled=True),
    )
    local_rows = query_rows.shape[0]
    tok_index = lax.axis_index("tok")
    tok_count = lax.axis_size("tok")
    previous = shifted(
        (key_rows[local_rows - WINDOW :], value_rows[local_rows - WINDOW :]), "tok", 1
    )
    window_key_rows = jnp.concatenate([previous[0], key_rows])
    window_value_rows = jnp.concatenate([previous[1], value_rows])
    block_rows = block_size()
    first_position = tok_index * local_rows

    def attend_block(block_index):
        offset = block_index * block_rows
        queries_here = lax.dynamic_slice_in_dim(query_rows, offset, block_rows, 0)
        keys_here = lax.dynamic_slice_in_dim(window_key_rows, offset, block_rows + WINDOW, 0)
        values_here = lax.dynamic_slice_in_dim(window_value_rows, offset, block_rows + WINDOW, 0)
        positions = first_position + offset + jnp.arange(block_rows, dtype=jnp.int32)
        key_positions = (
            first_position + offset - WINDOW + jnp.arange(block_rows + WINDOW, dtype=jnp.int32)
        )
        return attend(queries_here, keys_here, values_here, positions, key_positions)

    attended = lax.map(attend_block, jnp.arange(local_rows // block_rows, dtype=jnp.int32)).reshape(
        local_rows, DH
    )
    attended = rms_norm(attended)
    weights = fast_weights[0]
    rate_rows = token_rates[0]
    gate_value = across(key_rows, weights[:, :DH])
    up_value = across(key_rows, weights[:, DH : 2 * DH])
    gate_silu, gate_slope = silu_parts(gate_value)
    hidden = (gate_silu * up_value).astype(jnp.bfloat16)
    target = (-rate_rows[:, None] * value_rows.astype(jnp.float32)).astype(jnp.bfloat16)
    back_grad = across(target, weights[:, 2 * DH :])
    gate_grad = (back_grad * up_value * gate_slope).astype(jnp.bfloat16)
    up_grad = (back_grad * gate_silu).astype(jnp.bfloat16)
    owned_rows = FH // tok_count

    def outer(left):
        return lax.dot_general(
            left,
            key_rows if left is not hidden else target,
            (((0,), (0,)), ((), ())),
            preferred_element_type=jnp.float32,
        )

    gradient = (
        lax.psum(
            jnp.concatenate([outer(gate_grad), outer(up_grad), outer(hidden)], axis=1).astype(
                jnp.bfloat16
            ),
            "tok",
        )
        .astype(jnp.float32)
        .reshape(FH, 3, DH)
    )
    squares = jnp.sum(gradient * gradient, axis=(0, 2))
    iterate = (gradient * lax.rsqrt(squares + epsilon)[None, :, None]).astype(jnp.bfloat16)
    for repeat_index in range(NS_STEPS):
        gram_matrix = jnp.einsum(
            "fjd,fje->jde", iterate, iterate, preferred_element_type=jnp.float32
        ).astype(jnp.bfloat16)
        iterate = polish(iterate, gram_matrix)
    updated = (
        (weights.reshape(FH, 3, DH).astype(jnp.float32) - iterate.astype(jnp.float32))
        .astype(jnp.bfloat16)
        .reshape(FH, 3 * DH)
    )
    owned_weights = lax.dynamic_slice_in_dim(updated, tok_index * owned_rows, owned_rows, 0)
    applied = apply_rows(query_rows, updated)
    combined = (attended + rms_norm(applied)).astype(jnp.bfloat16)
    combined = lax.all_to_all(combined, "head", split_axis=0, concat_axis=1, tiled=True)
    return (combined, owned_weights[None])


def solution(mesh):
    return jax.shard_map(
        per_device,
        mesh=mesh,
        in_specs=(
            P(("tok", "head"), None),
            P(("tok", "head"), None),
            P(("tok", "head"), None),
            P("head", "tok"),
            P("head", None, None),
        ),
        out_specs=(P(("tok", "head"), None), P("head", "tok", None)),
        check_vma=False,
    )
```

profile of v0, /device:TPU:1, one launch (start us, length us, event | category | flops | bytes accessed | tf_op | source)
XLA Modules:
  0.0 215.3 jit_solution(3780948227441279132)
XLA Ops:
  7.2 2.4 %copy.76 = bf16[16,16,8,256]{3,2,0,1:T(8,128)(2,1)} copy(bf16[16,16,8,256]{3,2,1,0:T(8,128)(2,1)} %bitcast.147) | data formatting | bytes 2097152 | tf_op jit(solution)/shard_map/all_to_all | solution.py:75
  9.6 7.3 %all-to-all-start.1 = ((bf16[128,16,256]{2,0,1:T(8,128)(2,1)}), bf16[128,16,256]{2,0,1:T(8,128)(2,1)S(1)}, u32[]{:S(2)}, u32[]{:S(2)}) async-start(bf16[128,16,256]{2,0,1:T(8,128)(2,1)} %bitcast.121), calls=%async_computation.1 | async-start | bytes 2097152 | tf_op jit(solution)/shard_map/all_to_all | solution.py:75
  16.9 1.1 copy.75
  18.0 22.0 %all-to-all-done.1 = bf16[128,16,256]{2,0,1:T(8,128)(2,1)S(1)} async-done(((bf16[128,16,256]{2,0,1:T(8,128)(2,1)}), bf16[128,16,256]{2,0,1:T(8,128)(2,1)S(1)}, u32[]{:S(2)}, u32[]{:S(2)}) %all-to-all-start.1) | async-done | bytes 1048608 | tf_op jit(solution)/shard_map/all_to_all | solution.py:75
  40.1 6.5 %all-to-all-start.2 = ((bf16[128,16,256]{2,0,1:T(8,128)(2,1)}), bf16[128,16,256]{2,0,1:T(8,128)(2,1)S(1)}, u32[]{:S(2)}, u32[]{:S(2)}) async-start(bf16[128,16,256]{2,0,1:T(8,128)(2,1)} %bitcast.120), calls=%async_computation.2 | async-start | bytes 2097152 | tf_op jit(solution)/shard_map/all_to_all | solution.py:76
  46.6 1.4 copy.32
  48.0 2.3 %copy.77 = bf16[16,16,8,256]{3,2,0,1:T(8,128)(2,1)} copy(bf16[16,16,8,256]{3,2,1,0:T(8,128)(2,1)} %bitcast.149) | data formatting | bytes 2097152 | tf_op jit(solution)/shard_map/all_to_all | solution.py:74
  50.3 2.7 %fusion.69 = f32[2048,512]{1,0:T(8,128)} fusion(bf16[2048,256]{1,0:T(8,128)(2,1)S(1)} %bitcast.127, bf16[512,768]{1,0:T(8,128)(2,1)S(1)} %bitcast.142), kind=kOutput, calls=%fused_computation.109 | convolution fusion | flops 536870912 | bytes 5505024 | tf_op jit(solution)/shard_map/dot_general | solution.py:38
  53.1 2.7 %fusion.71 = f32[2048,512]{1,0:T(8,128)} fusion(bf16[2048,256]{1,0:T(8,128)(2,1)S(1)} %bitcast.128, bf16[512,768]{1,0:T(8,128)(2,1)S(1)} %bitcast.143), kind=kOutput, calls=%fused_computation.111 | convolution fusion | flops 536870912 | bytes 5505024 | tf_op jit(solution)/shard_map/dot_general | solution.py:38
  55.7 14.0 %all-to-all-done.2 = bf16[128,16,256]{2,0,1:T(8,128)(2,1)S(1)} async-done(((bf16[128,16,256]{2,0,1:T(8,128)(2,1)}), bf16[128,16,256]{2,0,1:T(8,128)(2,1)S(1)}, u32[]{:S(2)}, u32[]{:S(2)}) %all-to-all-start.2) | async-done | bytes 1048608 | tf_op jit(solution)/shard_map/all_to_all | solution.py:76
  69.8 6.5 %all-to-all-start = ((bf16[128,16,256]{2,0,1:T(8,128)(2,1)}), bf16[128,16,256]{2,0,1:T(8,128)(2,1)S(1)}, u32[]{:S(2)}, u32[]{:S(2)}) async-start(bf16[128,16,256]{2,0,1:T(8,128)(2,1)} %bitcast.139), calls=%async_computation | async-start | bytes 2097152 | tf_op jit(solution)/shard_map/all_to_all | solution.py:74
  76.3 1.9 fusion.53
  78.6 4.2 %fusion.38 = bf16[512,256]{0,1:T(8,128)(2,1)S(1)} fusion(bf16[2048,256]{1,0:T(8,128)(2,1)S(1)} %bitcast.129, f32[2048,512]{1,0:T(8,128)S(1)} %copy-done, f32[2048,512]{1,0:T(8,128)S(1)} %fusion.53, f32[2048,512]{1,0:T(8,128)} %fusion.71), kind=kOutput, calls=%fused_computation.77 | convolution fusion | flops 547487744 | bytes 13893632 | tf_op jit(solution)/shard_map/dot_general | solution.py:117
  82.8 1.7 fusion.39
  84.6 0.9 slice.40
  85.4 3.9 %collective-permute-start = (bf16[1024,256]{1,0:T(8,128)(2,1)}, bf16[1024,256]{1,0:T(8,128)(2,1)}, u32[]{:S(2)}, u32[]{:S(2)}) collective-permute-start(bf16[1024,256]{1,0:T(8,128)(2,1)} %bitcast.5), channel_id=1, source_target_pairs={{0,16},{1,17},{2,18},{3,19},{4,20},{5,21},{6,22},{7,23},{8,24},{9,... | collective-permute-start | bytes 1572872 | tf_op jit(solution)/shard_map/ppermute | solution.py:21
  90.2 2.1 collective-permute-start.1
  92.2 1.5 fusion.40
  93.7 0.9 pad_maximum_fusion.2
  94.7 5.3 %collective-permute-done = bf16[1024,256]{1,0:T(8,128)(2,1)} collective-permute-done((bf16[1024,256]{1,0:T(8,128)(2,1)}, bf16[1024,256]{1,0:T(8,128)(2,1)}, u32[]{:S(2)}, u32[]{:S(2)}) %collective-permute-start) | collective-permute-done | bytes 524320 | tf_op jit(solution)/shard_map/ppermute | solution.py:21
  100.0 2.4 %pad_maximum_fusion = bf16[3072,256]{1,0:T(8,128)(2,1)} fusion(bf16[2048,256]{1,0:T(8,128)(2,1)S(1)} %bitcast.132, bf16[1024,256]{1,0:T(8,128)(2,1)} %collective-permute-done), kind=kLoop, calls=%fused_computation.41 | loop fusion | flops 3145728 | bytes 3145728 | tf_op jit(solution)/shard_map/concatenate | solution.py:84
  102.4 17.3 %collective-permute-done.1 = bf16[1024,256]{1,0:T(8,128)(2,1)} collective-permute-done((bf16[1024,256]{1,0:T(8,128)(2,1)}, bf16[1024,256]{1,0:T(8,128)(2,1)}, u32[]{:S(2)}, u32[]{:S(2)}) %collective-permute-start.1) | collective-permute-done | bytes 524320 | tf_op jit(solution)/shard_map/ppermute | solution.py:21
  119.7 2.3 %pad_maximum_fusion.1 = bf16[3072,256]{1,0:T(8,128)(2,1)} fusion(bf16[2048,256]{1,0:T(8,128)(2,1)S(1)} %bitcast.136, bf16[1024,256]{1,0:T(8,128)(2,1)} %collective-permute-done.1), kind=kLoop, calls=%fused_computation.42 | loop fusion | flops 3145728 | bytes 3145728 | tf_op jit(solution)/shard_map/concatenate | solution.py:85
  122.0 26.7 %while.12 = (s32[]{:T(128)}, f32[4,512,256]{2,1,0:T(8,128)}, s32[4]{0:T(128)S(1)}, s32[]{:T(128)}, bf16[2048,256]{1,0:T(8,128)(2,1)S(1)}, /*index=5*/bf16[3072,2...) while((s32[]{:T(128)}, f32[4,512,256]{2,1,0:T(8,128)}, ...), condition=%wide.region_3.4_spmd, body=%wide.region_0.3_spmd.sunk | while | flops 815534080 | bytes 18120988 | solution.py:100
  123.3 2.4 %fusion.126 = (f32[512]{0:T(512)S(1)}, f32[512,1536]{1,0:T(8,128)S(1)}) fusion(bf16[3072,256]{1,0:T(8,128)(2,1)} %get-tuple-element.188, s32[]{:T(128)S(6)} %select_n.27, bf16[2048,256]{1,0:T(8,128)(2,1)S(1)} %get-tuple-element.187, s32[]{:T(128)S(6)} %select_n.28, pred[1536]{0:T(1024)(128)(4,1)S(1)} %broadcast_compare_fusion.2, ...), kind=kOutput, calls=%fused_computation.132.clone.1 | convolution fusion | flops 408944128 | bytes 4208648 | tf_op jit(solution)/shard_map/while/body/eval_jaxpr/dot_general | solution.py:51
  126.3 0.9 copy-done.7
  127.1 1.6 fusion.128
  130.0 2.4 %fusion.126 = (f32[512]{0:T(512)S(1)}, f32[512,1536]{1,0:T(8,128)S(1)}) fusion(bf16[3072,256]{1,0:T(8,128)(2,1)} %get-tuple-element.188, s32[]{:T(128)S(6)} %select_n.27, bf16[2048,256]{1,0:T(8,128)(2,1)S(1)} %get-tuple-element.187, s32[]{:T(128)S(6)} %select_n.28, pred[1536]{0:T(1024)(128)(4,1)S(1)} %broadcast_compare_fusion.2, ...), kind=kOutput, calls=%fused_computation.132.clone.1 | convolution fusion | flops 408944128 | bytes 4208648 | tf_op jit(solution)/shard_map/while/body/eval_jaxpr/dot_general | solution.py:51
  133.8 1.6 fusion.128
  136.7 2.4 %fusion.126 = (f32[512]{0:T(512)S(1)}, f32[512,1536]{1,0:T(8,128)S(1)}) fusion(bf16[3072,256]{1,0:T(8,128)(2,1)} %get-tuple-element.188, s32[]{:T(128)S(6)} %select_n.27, bf16[2048,256]{1,0:T(8,128)(2,1)S(1)} %get-tuple-element.187, s32[]{:T(128)S(6)} %select_n.28, pred[1536]{0:T(1024)(128)(4,1)S(1)} %broadcast_compare_fusion.2, ...), kind=kOutput, calls=%fused_computation.132.clone.1 | convolution fusion | flops 408944128 | bytes 4208648 | tf_op jit(solution)/shard_map/while/body/eval_jaxpr/dot_general | solution.py:51
  140.5 1.5 fusion.128
  143.3 2.5 %fusion.126 = (f32[512]{0:T(512)S(1)}, f32[512,1536]{1,0:T(8,128)S(1)}) fusion(bf16[3072,256]{1,0:T(8,128)(2,1)} %get-tuple-element.188, s32[]{:T(128)S(6)} %select_n.27, bf16[2048,256]{1,0:T(8,128)(2,1)S(1)} %get-tuple-element.187, s32[]{:T(128)S(6)} %select_n.28, pred[1536]{0:T(1024)(128)(4,1)S(1)} %broadcast_compare_fusion.2, ...), kind=kOutput, calls=%fused_computation.132.clone.1 | convolution fusion | flops 408944128 | bytes 4208648 | tf_op jit(solution)/shard_map/while/body/eval_jaxpr/dot_general | solution.py:51
  147.2 1.5 fusion.128
  148.7 1.9 multiply_reduce_fusion.1
  150.7 1.4 multiply_reduce_fusion.2
  152.3 1.9 convolution_convert_fusion.4
  156.9 0.9 copy-done.4
  157.8 1.1 convolution_convert_fusion.1
  158.9 2.5 %fusion.23 = bf16[512,3,256]{0,2,1:T(8,128)(2,1)S(1)} fusion(bf16[512,3,256]{0,2,1:T(8,128)(2,1)} %copy-done.4, bf16[3,256,256]{2,1,0:T(8,128)(2,1)} %convolution_convert_fusion.1), kind=kOutput, calls=%fused_computation.46 | convolution fusion | flops 304545792 | bytes 1966080 | tf_op jit(solution)/shard_map/fjd,jde->fje/dot_general | solution.py:68
  161.4 1.2 convolution_convert_fusion
  162.5 3.1 %subtract_convert_fusion = bf16[512,3,256]{0,2,1:T(8,128)(2,1)} fusion(f32[512,3,256]{0,2,1:T(8,128)S(1)} %bitcast.138, bf16[512,3,256]{0,2,1:T(8,128)(2,1)S(1)} %fusion.23, bf16[3,256,256]{2,1,0:T(8,128)(2,1)} %convolution_convert_fusion), kind=kOutput, calls=%fused_computation.53 | convolution fusion | flops 305725440 | bytes 3538944 | tf_op jit(solution)/shard_map/fjd,jde->fje/dot_general | solution.py:68
  165.6 3.6 %fusion.67 = f32[512,2048]{0,1:T(8,128)} fusion(bf16[2048,256]{1,0:T(8,128)(2,1)S(1)} %get-tuple-element.200, bf16[512,768]{0,1:T(8,128)(2,1)} %bitcast.144), kind=kOutput, calls=%fused_computation.107 | convolution fusion | flops 536870912 | bytes 5505024 | tf_op jit(solution)/shard_map/dot_general | solution.py:38
  169.2 5.5 %multiply_reduce_fusion = (f32[2048]{0:T(1024)S(1)}, f32[2048,256]{1,0:T(8,128)}) fusion(bf16[512,768]{0,1:T(8,128)(2,1)} %bitcast.145, f32[512,2048]{0,1:T(8,128)} %fusion.67, bf16[2048,256]{1,0:T(8,128)(2,1)S(1)} %get-tuple-element.200), kind=kOutput, calls=%fused_computation.37 | convolution fusion | flops 1081079808 | bytes 7872512 | tf_op jit(solution)/shard_map/dot_general | solution.py:47
  174.7 2.8 %fusion.20 = bf16[2048,256]{1,0:T(8,128)(2,1)} fusion(f32[4,512,256]{2,1,0:T(8,128)S(1)} %copy-done.2, f32[2048,256]{1,0:T(8,128)} %get-tuple-element.109, f32[2048]{0:T(1024)S(1)} %add_rsqrt_fusion, f32[2048]{0:T(1024)S(1)} %bitcast.154), kind=kLoop, calls=%fused_computation.36 | loop fusion | flops 2097152 | bytes 5259264 | tf_op jit(solution)/shard_map/convert_element_type | solution.py:148
  177.5 6.7 %all-to-all-start.3 = ((bf16[16,128,256]{2,1,0:T(8,128)(2,1)}), bf16[16,128,256]{2,1,0:T(8,128)(2,1)S(1)}, u32[]{:S(2)}, u32[]{:S(2)}) async-start(bf16[16,128,256]{2,1,0:T(8,128)(2,1)} %bitcast.26), calls=%async_computation.3 | async-start | bytes 2097152 | tf_op jit(solution)/shard_map/all_to_all | solution.py:149
  184.2 0.9 copy.50
  185.1 22.2 %all-to-all-done.3 = bf16[16,128,256]{2,1,0:T(8,128)(2,1)S(1)} async-done(((bf16[16,128,256]{2,1,0:T(8,128)(2,1)}), bf16[16,128,256]{2,1,0:T(8,128)(2,1)S(1)}, u32[]{:S(2)}, u32[]{:S(2)}) %all-to-all-start.3) | async-done | bytes 1048608 | tf_op jit(solution)/shard_map/all_to_all | solution.py:149
  207.4 1.1 copy.70
  (66 shorter events, 11.4 us)
Async XLA Ops:
  7.2 9.7 %copy-start.8 = (bf16[128,4096]{1,0:T(8,128)(2,1)S(1)}, bf16[128,4096]{1,0:T(8,128)(2,1)}, u32[]{:S(2)}) copy-start(bf16[128,4096]{1,0:T(8,128)(2,1)} %param.9) | copy-start | bytes 3145732
  9.6 30.5 %all-to-all-start.1 = ((bf16[128,16,256]{2,0,1:T(8,128)(2,1)}), bf16[128,16,256]{2,0,1:T(8,128)(2,1)S(1)}, u32[]{:S(2)}, u32[]{:S(2)}) async-start(bf16[128,16,256]{2,0,1:T(8,128)(2,1)} %bitcast.121), calls=%async_computation.1 | async-start | bytes 2097152 | tf_op jit(solution)/shard_map/all_to_all | solution.py:75
  16.9 29.7 %copy-start.10 = (f32[1,2048]{1,0:T(1,128)S(1)}, f32[1,2048]{1,0:T(1,128)}, u32[]{:S(2)}) copy-start(f32[1,2048]{1,0:T(1,128)} %param.10) | copy-start | bytes 24580
  16.9 29.7 %copy-start.5 = (bf16[1,512,768]{2,1,0:T(8,128)(2,1)S(1)}, bf16[1,512,768]{2,1,0:T(8,128)(2,1)}, u32[]{:S(2)}) copy-start(bf16[1,512,768]{2,1,0:T(8,128)(2,1)} %param.11) | copy-start | bytes 2359300
  40.1 29.7 %all-to-all-start.2 = ((bf16[128,16,256]{2,0,1:T(8,128)(2,1)}), bf16[128,16,256]{2,0,1:T(8,128)(2,1)S(1)}, u32[]{:S(2)}, u32[]{:S(2)}) async-start(bf16[128,16,256]{2,0,1:T(8,128)(2,1)} %bitcast.120), calls=%async_computation.2 | async-start | bytes 2097152 | tf_op jit(solution)/shard_map/all_to_all | solution.py:76
  69.8 52.2 %all-to-all-start = ((bf16[128,16,256]{2,0,1:T(8,128)(2,1)}), bf16[128,16,256]{2,0,1:T(8,128)(2,1)S(1)}, u32[]{:S(2)}, u32[]{:S(2)}) async-start(bf16[128,16,256]{2,0,1:T(8,128)(2,1)} %bitcast.139), calls=%async_computation | async-start | bytes 2097152 | tf_op jit(solution)/shard_map/all_to_all | solution.py:74
  76.3 74.4 %all-reduce.2.cloned.1.call-start = ((), (), s32[]{:S(2)}) async-start(), calls=%async_computation.4 | async-start | bytes 1572864 | tf_op jit(solution)/shard_map/psum | solution.py:125
  76.3 2.3 %copy-start = (f32[2048,512]{1,0:T(8,128)S(1)}, f32[2048,512]{1,0:T(8,128)}, u32[]{:S(2)}) copy-start(f32[2048,512]{1,0:T(8,128)} %fusion.69) | copy-start | bytes 12582916
  78.6 4.2 %copy-start.1 = (f32[2048,512]{1,0:T(8,128)S(1)}, f32[2048,512]{1,0:T(8,128)}, u32[]{:S(2)}) copy-start(f32[2048,512]{1,0:T(8,128)} %fusion.71) | copy-start | bytes 12582916
  85.4 14.6 %collective-permute-start = (bf16[1024,256]{1,0:T(8,128)(2,1)}, bf16[1024,256]{1,0:T(8,128)(2,1)}, u32[]{:S(2)}, u32[]{:S(2)}) collective-permute-start(bf16[1024,256]{1,0:T(8,128)(2,1)} %bitcast.5), channel_id=1, source_target_pairs={{0,16},{1,17},{2,18},{3,19},{4,20},{5,21},{6,22},{7,23},{8,24},{9,... | collective-permute-start | bytes 1572872 | tf_op jit(solution)/shard_map/ppermute | solution.py:21
  90.2 29.5 %collective-permute-start.1 = (bf16[1024,256]{1,0:T(8,128)(2,1)}, bf16[1024,256]{1,0:T(8,128)(2,1)}, u32[]{:S(2)}, u32[]{:S(2)}) collective-permute-start(bf16[1024,256]{1,0:T(8,128)(2,1)} %bitcast.8), channel_id=1, source_target_pairs={{0,16},{1,17},{2,18},{3,19},{4,20},{5,21},{6,22},{7,23},{8,24},{9,... | collective-permute-start | bytes 1572872 | tf_op jit(solution)/shard_map/ppermute | solution.py:21
  125.7 1.5 copy-start.7
  132.4 1.4 copy-start.7
  139.1 1.4 copy-start.7
  145.8 1.4 copy-start.7
  150.7 3.5 %copy-start.9 = (bf16[512,768]{0,1:T(8,128)(2,1)S(1)}, bf16[512,768]{0,1:T(8,128)(2,1)}, u32[]{:S(2)}) copy-start(bf16[512,768]{0,1:T(8,128)(2,1)} %all-reduce.2.cloned.1.call-done) | copy-start | bytes 2359300
  156.9 0.9 copy-start.4
  158.9 3.6 %copy-start.3 = (f32[1,512,768]{1,2,0:T(8,128)S(1)}, f32[1,512,768]{1,2,0:T(8,128)}, u32[]{:S(2)}) copy-start(f32[1,512,768]{1,2,0:T(8,128)} %copy.32) | copy-start | bytes 4718596
  169.2 5.5 %copy-start.2 = (f32[4,512,256]{2,1,0:T(8,128)S(1)}, f32[4,512,256]{2,1,0:T(8,128)}, u32[]{:S(2)}) copy-start(f32[4,512,256]{2,1,0:T(8,128)} %get-tuple-element.91) | copy-start | bytes 6291460
  177.5 6.7 %copy-start.6 = (bf16[512,3,256]{0,2,1:T(8,128)(2,1)S(1)}, bf16[512,3,256]{0,2,1:T(8,128)(2,1)}, u32[]{:S(2)}) copy-start(bf16[512,3,256]{0,2,1:T(8,128)(2,1)} %subtract_convert_fusion) | copy-start | bytes 2359300
  177.5 29.9 %all-to-all-start.3 = ((bf16[16,128,256]{2,1,0:T(8,128)(2,1)}), bf16[16,128,256]{2,1,0:T(8,128)(2,1)S(1)}, u32[]{:S(2)}, u32[]{:S(2)}) async-start(bf16[16,128,256]{2,1,0:T(8,128)(2,1)} %bitcast.26), calls=%async_computation.3 | async-start | bytes 2097152 | tf_op jit(solution)/shard_map/all_to_all | solution.py:149
Sparse Core Ops, SparseCore 0:
  94.8 42.8 all-reduce.1
where the time goes:
time: 218 us; the launch traced here: 215 us
  waiting for transfers between devices  80.9 us (37%)
  matrix products  52 us (24%)
  starting transfers between devices  33.1 us (15%)
  local copies, waits for them, and re-layouts  18 us (8%)
  other arithmetic  14.3 us (7%)
  between operations  14.3 us (7%)
  loops' own time  2.77 us (1%)
    ppermute x2, waiting for transfers between devices, shifted(): lax.ppermute(value, axis, [(source, source + steps) for source in range(f...  22.6 us
    all_to_all x1, waiting for transfers between devices, per_device(): lax.all_to_all(combined, 'head', split_axis=0, concat_axis=1, tiled=True)  22.2 us
    all_to_all x1, waiting for transfers between devices, per_device(): lax.all_to_all(key_states, 'head', split_axis=1, concat_axis=0, tiled=True)  22 us
    all_to_all x1, waiting for transfers between devices, per_device(): lax.all_to_all(value_states, 'head', split_axis=1, concat_axis=0, tiled=T...  14 us
    dot_general x4, matrix products, across(): lax.dot_general(inputs, weight_rows, (((1,), (1,)), ((), ())), preferred_...  10.8 us
    dot_general x4, matrix products, attend(): jnp.dot(query_rows, key_rows.T, preferred_element_type=jnp.float32)  9.75 us
    dot_general x3, matrix products, outer(): lax.dot_general(left, key_rows if left is not hidden else target, (((0,),...  7.43 us
    dot_general x5, matrix products, polish(): jnp.einsum('fjd,jde->fje', iterate, polynomial, preferred_element_type=jn...  7.37 us
  transfers between devices with their start and end apart: 7, of which 5 were waited for; matrix products, arithmetic and copies ran while one was open for 23% of the time, Pallas kernels for 0%

commit v1 on v0

v1 whole, which is shorter than its diff:
```python
import functools

import jax
import jax.numpy as jnp
from jax import lax
from jax.experimental import pallas as pl
from jax.experimental.pallas import tpu as pltpu
from jax.sharding import PartitionSpec as P

DH = 256
FH = 512
WINDOW = 1024
NS_STEPS = 5

coef_linear = 3.4445
coef_cubic = -4.775
coef_quintic = 2.0315
epsilon = 1e-06
LOG2E = 1.4426950408889634
MASKED = -1e30
MESH = pl.DeviceIdType.MESH


def dot_nt(left, right):
    return lax.dot_general(
        left, right, (((1,), (1,)), ((), ())), preferred_element_type=jnp.float32
    )


def dot_nn(left, right):
    return lax.dot_general(
        left, right, (((1,), (0,)), ((), ())), preferred_element_type=jnp.float32
    )


def rms_norm(values):
    return values * lax.rsqrt(jnp.mean(values * values, axis=-1, keepdims=True) + epsilon)


def sigmoid(values):
    return 1.0 / (1.0 + jnp.exp(-values))


def turned(values):
    return values.astype(jnp.float32).T.astype(jnp.bfloat16)


def layer_kernel(
    n_tok, n_head, q_hbm, k_hbm, v_hbm, rate_ref, w_ref,
    out_hbm, neww_ref,
    kw, vw, qw, rs, att, acc, grads, zs, wnew, obuf,
    own_sem, k_send, k_recv, v_send, v_recv, q_send, q_recv, o_send, o_recv,
    hk_send, hk_recv, hv_send, hv_recv, g_send, g_recv,
):
    tok = lax.axis_index("tok")
    me = lax.axis_index("head")
    rd = q_hbm.shape[0]
    rg = 2 * rd
    groups = n_head // 2
    halo_groups = WINDOW // rg
    mine = lax.div(me, 2)
    early = max(groups - 2, 1)

    barrier = pltpu.get_barrier_semaphore()

    @pl.loop(1, n_head)
    def _(step):
        pl.semaphore_signal(
            barrier, inc=1, device_id=(tok, lax.rem(me + step, n_head)), device_id_type=MESH
        )

    @pl.loop(1, n_tok)
    def _(step):
        pl.semaphore_signal(
            barrier, inc=1, device_id=(lax.rem(tok + step, n_tok), me), device_id_type=MESH
        )

    def rows_of(index, size, base=0):
        return pl.ds(pl.multiple_of(base + index * size, size), size)

    def cols_of(index):
        return pl.ds(pl.multiple_of(index * DH, DH), DH)

    def scatter(src, dst, base, send, recv, source, target):
        return pltpu.make_async_remote_copy(
            src_ref=src.at[:, cols_of(target)],
            dst_ref=dst.at[rows_of(source, rd, base)],
            send_sem=send.at[target],
            recv_sem=recv.at[source],
            device_id=(tok, target),
            device_id_type=MESH,
        )

    def k_copy(source, target):
        return scatter(k_hbm, kw, WINDOW, k_send, k_recv, source, target)

    def v_copy(source, target):
        return scatter(v_hbm, vw, WINDOW, v_send, v_recv, source, target)

    def q_copy(source, target):
        return scatter(q_hbm, qw, 0, q_send, q_recv, source, target)

    def o_copy(source, target):
        return pltpu.make_async_remote_copy(
            src_ref=obuf.at[rows_of(target, rd)],
            dst_ref=out_hbm.at[:, cols_of(source)],
            send_sem=o_send.at[target],
            recv_sem=o_recv.at[source],
            device_id=(tok, target),
            device_id_type=MESH,
        )

    own_copies = (
        pltpu.make_async_copy(
            k_hbm.at[:, cols_of(me)], kw.at[rows_of(me, rd, WINDOW)], own_sem.at[0]
        ),
        pltpu.make_async_copy(
            v_hbm.at[:, cols_of(me)], vw.at[rows_of(me, rd, WINDOW)], own_sem.at[1]
        ),
        pltpu.make_async_copy(q_hbm.at[:, cols_of(me)], qw.at[rows_of(me, rd)], own_sem.at[2]),
    )
    for copy in own_copies:
        copy.start()

    pl.semaphore_wait(barrier, n_head - 1 + n_tok - 1)

    @pl.loop(1, n_head)
    def _(step):
        target = lax.rem(me + step, n_head)
        k_copy(me, target).start()
        v_copy(me, target).start()

    @pl.loop(1, n_head)
    def _(step):
        q_copy(me, lax.rem(me + step, n_head)).start()

    acc[...] = jnp.zeros_like(acc)

    @pl.when(tok == 0)
    def _():
        kw[0:WINDOW, :] = jnp.zeros((WINDOW, DH), jnp.bfloat16)
        vw[0:WINDOW, :] = jnp.zeros((WINDOW, DH), jnp.bfloat16)

    @pl.loop(0, rs.shape[0] // 128)
    def _(index):
        part = rate_ref[:, rows_of(index, 128)]
        rs[rows_of(index, 128), :] = -jnp.broadcast_to(part, (128, 128)).T

    for copy in own_copies:
        copy.wait()

    def halo_copy(local, halo, send, recv, part):
        return pltpu.make_async_remote_copy(
            src_ref=local.at[rows_of(part + groups, rg)],
            dst_ref=halo.at[rows_of(part, rg)],
            send_sem=send.at[part],
            recv_sem=recv.at[part],
            device_id=(jnp.minimum(tok + 1, n_tok - 1), me),
            device_id_type=MESH,
        )

    def hk_copy(part):
        return halo_copy(kw, kw, hk_send, hk_recv, part)

    def hv_copy(part):
        return halo_copy(vw, vw, hv_send, hv_recv, part)

    def group_at(step):
        return lax.rem(mine - step + groups, groups)

    def wait_group(group, copies):
        for core in range(2):
            source = group * 2 + core

            @pl.when(source != me)
            def _():
                for copy in copies:
                    copy(source, me).wait_recv()

    @pl.loop(0, groups)
    def _(step):
        group = group_at(step)
        wait_group(group, (k_copy, v_copy))
        part = group - (groups - halo_groups)

        @pl.when(jnp.logical_and(part >= 0, tok < n_tok - 1))
        def _():
            hk_copy(part).start()
            hv_copy(part).start()

        keys = kw[rows_of(group, rg, WINDOW), :]
        values = vw[rows_of(group, rg, WINDOW), :].astype(jnp.float32)
        rates = rs[rows_of(group, rg), :]
        target = jnp.concatenate(
            [values[:, :128] * rates, values[:, 128:] * rates], axis=1
        )
        target = target.astype(jnp.bfloat16)
        gate = dot_nt(keys, w_ref[0, :, 0:DH])
        up = dot_nt(keys, w_ref[0, :, DH : 2 * DH])
        back = dot_nt(target, w_ref[0, :, 2 * DH :])
        sig = sigmoid(gate)
        silu = gate * sig
        slope = sig * (1.0 + gate * (1.0 - sig))
        hidden = (silu * up).astype(jnp.bfloat16)
        gate_grad = (back * up * slope).astype(jnp.bfloat16)
        up_grad = (back * silu).astype(jnp.bfloat16)
        keys_t = turned(keys)
        acc[0] += dot_nn(keys_t, gate_grad)
        acc[1] += dot_nn(keys_t, up_grad)
        acc[2] += dot_nn(turned(target), hidden)

    def g_copy(source, target):
        return pltpu.make_async_remote_copy(
            src_ref=grads.at[source],
            dst_ref=grads.at[source],
            send_sem=g_send.at[target],
            recv_sem=g_recv.at[source],
            device_id=(target, me),
            device_id_type=MESH,
        )

    grads[tok] = acc[...].astype(jnp.bfloat16)

    @pl.loop(1, n_tok)
    def _(step):
        g_copy(tok, lax.rem(tok + step, n_tok)).start()

    @pl.when(tok > 0)
    def _():
        @pl.loop(0, halo_groups)
        def _(part):
            hk_copy(part).wait_recv()
            hv_copy(part).wait_recv()

    row = lax.broadcasted_iota(jnp.int32, (rg, rg), 0)
    col = lax.broadcasted_iota(jnp.int32, (rg, rg), 1)

    def attend(group):
        wait_group(group, (q_copy,))
        queries = qw[rows_of(group, rg), :]
        scores = []
        for chunk in range(halo_groups + 1):
            value = dot_nt(queries, kw[rows_of(group + chunk, rg), :])
            if chunk == 0:
                value = jnp.where(col > row, value, MASKED)
            if chunk == halo_groups:
                value = jnp.where(col <= row, value, MASKED)
            else:
                seen = jnp.logical_or(tok > 0, group + chunk >= halo_groups)
                value = value + jnp.where(seen, 0.0, MASKED)
            scores.append(value)
        highest = functools.reduce(jnp.maximum, scores)
        highest = jnp.max(highest, axis=1, keepdims=True)
        total = jnp.zeros((rg, rg), jnp.float32)
        result = jnp.zeros((rg, DH), jnp.float32)
        for chunk in range(halo_groups + 1):
            expo = jnp.exp2((scores[chunk] - highest) * (LOG2E * DH ** (-0.5)))
            total = total + expo
            result = result + dot_nn(
                expo.astype(jnp.bfloat16), vw[rows_of(group + chunk, rg), :]
            )
        result = result / jnp.sum(total, axis=1, keepdims=True)
        att[rows_of(group, rg), :] = rms_norm(result)

    @pl.loop(0, early)
    def _(step):
        attend(group_at(step))

    @pl.loop(1, n_tok)
    def _(step):
        g_copy(lax.rem(tok + step, n_tok), tok).wait_recv()

    for block in range(3):
        total = grads[0, block].astype(jnp.float32)
        for index in range(1, n_tok):
            total = total + grads[index, block].astype(jnp.float32)
        squares = jnp.sum(
            jnp.sum(total * total, axis=1, keepdims=True), axis=0, keepdims=True
        )
        zs[block] = (total * lax.rsqrt(squares + epsilon)).astype(jnp.bfloat16)

    @pl.loop(0, NS_STEPS)
    def _(step):
        blocks = [zs[block] for block in range(3)]
        grams = [dot_nt(z, z).astype(jnp.bfloat16) for z in blocks]
        polys = [
            (coef_cubic * a.astype(jnp.float32) + coef_quintic * dot_nn(a, a)).astype(
                jnp.bfloat16
            )
            for a in grams
        ]
        for block in range(3):
            zs[block] = (
                coef_linear * blocks[block].astype(jnp.float32)
                + dot_nn(polys[block], blocks[block])
            ).astype(jnp.bfloat16)

    for block in range(3):
        columns = slice(block * DH, (block + 1) * DH)
        wnew[:, columns] = (
            w_ref[0, :, columns].astype(jnp.float32) - zs[block].astype(jnp.float32).T
        ).astype(jnp.bfloat16)

    @pl.loop(1, groups + 1)
    def _(step):
        group = group_at(step)

        @pl.when(jnp.logical_and(step >= early, step < groups))
        def _():
            attend(group)

        queries = qw[rows_of(group, rg), :]
        gate = dot_nt(queries, wnew[:, 0:DH])
        up = dot_nt(queries, wnew[:, DH : 2 * DH])
        hidden = (gate * sigmoid(gate) * up).astype(jnp.bfloat16)
        applied = rms_norm(dot_nn(hidden, wnew[:, 2 * DH :]))
        obuf[rows_of(group, rg), :] = (att[rows_of(group, rg), :] + applied).astype(
            jnp.bfloat16
        )
        for core in range(2):
            target = group * 2 + core

            @pl.when(target != me)
            def _():
                o_copy(me, target).start()

    own_out = pltpu.make_async_copy(
        obuf.at[rows_of(me, rd)], out_hbm.at[:, cols_of(me)], own_sem.at[3]
    )
    own_out.start()
    owned = FH // n_tok
    neww_ref[0] = wnew[rows_of(tok, owned), :]

    @pl.loop(1, n_head)
    def _(step):
        target = lax.rem(me + step, n_head)
        k_copy(me, target).wait_send()
        v_copy(me, target).wait_send()
        q_copy(me, target).wait_send()
        o_copy(me, target).wait_send()

    @pl.loop(1, n_tok)
    def _(step):
        g_copy(tok, lax.rem(tok + step, n_tok)).wait_send()

    @pl.when(tok < n_tok - 1)
    def _():
        @pl.loop(0, halo_groups)
        def _(part):
            hk_copy(part).wait_send()
            hv_copy(part).wait_send()

    @pl.loop(1, n_head)
    def _(step):
        o_copy(lax.rem(me + step, n_head), me).wait_recv()

    own_out.wait()


def per_device(query_states, key_states, value_states, token_rates, fast_weights):
    n_tok = lax.axis_size("tok")
    n_head = lax.axis_size("head")
    rd, width = query_states.shape
    rows = rd * n_head
    halo_groups = WINDOW // (2 * rd)
    dma = pltpu.SemaphoreType.DMA
    heads_sems = [dma((n_head,))] * 8
    return pl.pallas_call(
        functools.partial(layer_kernel, n_tok, n_head),
        out_shape=(
            jax.ShapeDtypeStruct((rd, width), jnp.bfloat16),
            jax.ShapeDtypeStruct((1, FH // n_tok, 3 * DH), jnp.bfloat16),
        ),
        in_specs=[pl.BlockSpec(memory_space=pl.ANY)] * 3
        + [pl.BlockSpec(memory_space=pltpu.VMEM)] * 2,
        out_specs=(
            pl.BlockSpec(memory_space=pl.ANY),
            pl.BlockSpec(memory_space=pltpu.VMEM),
        ),
        scratch_shapes=[
            pltpu.VMEM((WINDOW + rows, DH), jnp.bfloat16),
            pltpu.VMEM((WINDOW + rows, DH), jnp.bfloat16),
            pltpu.VMEM((rows, DH), jnp.bfloat16),
            pltpu.VMEM((rows, 128), jnp.float32),
            pltpu.VMEM((rows, DH), jnp.float32),
            pltpu.VMEM((3, DH, FH), jnp.float32),
            pltpu.VMEM((n_tok, 3, DH, FH), jnp.bfloat16),
            pltpu.VMEM((3, DH, FH), jnp.bfloat16),
            pltpu.VMEM((FH, 3 * DH), jnp.bfloat16),
            pltpu.VMEM((rows, DH), jnp.bfloat16),
            dma((4,)),
            *heads_sems,
            dma((halo_groups,)),
            dma((halo_groups,)),
            dma((halo_groups,)),
            dma((halo_groups,)),
            dma((n_tok,)),
            dma((n_tok,)),
        ],
        compiler_params=pltpu.CompilerParams(
            collective_id=0, has_side_effects=True, vmem_limit_bytes=60 * 1024 * 1024
        ),
        name="layer",
    )(query_states, key_states, value_states, token_rates, fast_weights)


def solution(mesh):
    return jax.shard_map(
        per_device,
        mesh=mesh,
        in_specs=(
            P(("tok", "head"), None),
            P(("tok", "head"), None),
            P(("tok", "head"), None),
            P("head", "tok"),
            P("head", None, None),
        ),
        out_specs=(P(("tok", "head"), None), P("head", "tok", None)),
        check_vma=False,
    )
```

time: 218 us -> 117 us (0.54); the launches traced: 215 us -> 117 us
  Pallas kernels: 0 us -> 113 us
  waiting for transfers between devices: 80.9 us -> 0 us
  matrix products: 52 us -> 0 us
  starting transfers between devices: 33.1 us -> 0 us
  local copies, waits for them, and re-layouts: 18 us -> 3.09 us
  other arithmetic: 14.3 us -> 0 us
  between operations: 14.3 us -> 0.65 us
  loops' own time: 2.77 us -> 0 us
    pallas_call x0 -> x1, Pallas kernels: none -> 113 us  [per_device(): pl.pallas_call(functools.partial(layer_kernel, n_tok, n_head), out_shape=...]
    all_to_all x4 -> x0, waiting for transfers between devices: 58.3 us -> none  [the longest x1 22.2 us: per_device(): lax.all_to_all(combined, 'head', split_axis=0, concat_axis=1, tiled=True)]
    dot_general x26 -> x0, matrix products: 52 us -> none  [the longest x4 10.8 us: across(): lax.dot_general(inputs, weight_rows, (((1,), (1,)), ((), ())), preferred_...]
    all_to_all x4 -> x0, starting transfers between devices: 27.1 us -> none  [the longest x1 7.34 us: per_device(): lax.all_to_all(key_states, 'head', split_axis=1, concat_axis=0, tiled=True)]
    ppermute x2 -> x0, waiting for transfers between devices: 22.6 us -> none  [shifted(): lax.ppermute(value, axis, [(source, source + steps) for source in range(f...]
    all_to_all x4 -> x0, local copies, waits for them, and re-layouts: 6.88 us -> none  [the longest x1 2.39 us: per_device(): lax.all_to_all(key_states, 'head', split_axis=1, concat_axis=0, tiled=True)]
    ppermute x2 -> x0, starting transfers between devices: 6 us -> none  [shifted(): lax.ppermute(value, axis, [(source, source + steps) for source in range(f...]
    reduce_sum x7 -> x0, other arithmetic: 5.75 us -> none  [the longest x4 2.27 us: attend(): probs = (expo / jnp.sum(expo, axis=1, keepdims=True)).astype(jnp.bfloat16)]
  transfers between devices with their start and end apart: 7 -> 0, of which waited for: 5 -> 0; matrix products, arithmetic and copies ran while one was open for 23% -> 0% of each run, Pallas kernels for 0% -> 0%
where the time goes in v1:
time: 117 us
  Pallas kernels  113 us (97%)
  local copies, waits for them, and re-layouts  3.09 us (3%)
    pallas_call x1, Pallas kernels, per_device(): pl.pallas_call(functools.partial(layer_kernel, n_tok, n_head), out_shape=...  113 us
    unnamed x4, local copies, waits for them, and re-layouts  3.09 us

profile of v1, /device:TPU:1, one launch (start us, length us, event | category | flops | bytes accessed | tf_op | source)
XLA Modules:
  0.0 116.7 jit_solution(6384914826876348036)
XLA Ops:
  0.6 113.0 %layer.1 = (bf16[128,4096]{1,0:T(8,128)(2,1)}, bf16[1,256,768]{2,1,0:T(8,128)(2,1)}) custom-call(bf16[128,4096]{1,0:T(8,128)(2,1)} %q_hbm.1, bf16[128,4096]{1,0:T(8,128)(2,1)} %k_hbm.1, bf16[128,4096]{1,0:T(8,128)(2,1)} %v_hbm.1, f32[1,2048]{1,0:T(1,128)} %rate_ref.1, bf16[1,512,768]{2,1,0:T(8,128)(2,1)} %w_ref.1), custom_call_target="tpu_custom_call" | custom-call | tf_op jit(solution)/shard_map/layer/pallas_call | solution.py:368
  113.6 0.0 copy-start
  113.6 2.3 %copy.9 = bf16[128,4096]{1,0:T(8,128)(2,1)} copy(bf16[128,4096]{1,0:T(8,128)(2,1)} %get-tuple-element.4) | data formatting | bytes 2097152
  116.0 0.0 copy-done
  116.0 0.7 copy.10
Async XLA Ops:
  113.6 2.4 %copy-start = (bf16[1,256,768]{2,1,0:T(8,128)(2,1)S(1)}, bf16[1,256,768]{2,1,0:T(8,128)(2,1)}, u32[]{:S(2)}) copy-start(bf16[1,256,768]{2,1,0:T(8,128)(2,1)} %get-tuple-element.5) | copy-start | bytes 1179652

commit v2 on v1

--- a/solution.py
+++ b/solution.py
@@ -48,9 +48,9 @@
 def layer_kernel(
     n_tok, n_head, q_hbm, k_hbm, v_hbm, rate_ref, w_ref,
     out_hbm, neww_ref,
-    kw, vw, qw, rs, att, acc, grads, zs, wnew, obuf,
+    kv, qw, rates, acc, zs, wnew, obuf,
     own_sem, k_send, k_recv, v_send, v_recv, q_send, q_recv, o_send, o_recv,
-    hk_send, hk_recv, hv_send, hv_recv, g_send, g_recv,
+    f_send, f_recv, r_send, r_recv,
 ):
     tok = lax.axis_index("tok")
     me = lax.axis_index("head")
@@ -59,7 +59,7 @@
     groups = n_head // 2
     halo_groups = WINDOW // rg
     mine = lax.div(me, 2)
-    early = max(groups - 2, 1)
+    first = tok * groups
 
     barrier = pltpu.get_barrier_semaphore()
 
@@ -75,8 +75,8 @@
             barrier, inc=1, device_id=(lax.rem(tok + step, n_tok), me), device_id_type=MESH
         )
 
-    def rows_of(index, size, base=0):
-        return pl.ds(pl.multiple_of(base + index * size, size), size)
+    def rows_of(index, size):
+        return pl.ds(pl.multiple_of(index * size, size), size)
 
     def cols_of(index):
         return pl.ds(pl.multiple_of(index * DH, DH), DH)
@@ -84,7 +84,7 @@
     def scatter(src, dst, base, send, recv, source, target):
         return pltpu.make_async_remote_copy(
             src_ref=src.at[:, cols_of(target)],
-            dst_ref=dst.at[rows_of(source, rd, base)],
+            dst_ref=dst.at[rows_of(base * n_head + source, rd)],
             send_sem=send.at[target],
             recv_sem=recv.at[source],
             device_id=(tok, target),
@@ -92,10 +92,10 @@
         )
 
     def k_copy(source, target):
-        return scatter(k_hbm, kw, WINDOW, k_send, k_recv, source, target)
+        return scatter(k_hbm, kv.at[0], tok, k_send, k_recv, source, target)
 
     def v_copy(source, target):
-        return scatter(v_hbm, vw, WINDOW, v_send, v_recv, source, target)
+        return scatter(v_hbm, kv.at[1], tok, v_send, v_recv, source, target)
 
     def q_copy(source, target):
         return scatter(q_hbm, qw, 0, q_send, q_recv, source, target)
@@ -112,10 +112,10 @@
 
     own_copies = (
         pltpu.make_async_copy(
-            k_hbm.at[:, cols_of(me)], kw.at[rows_of(me, rd, WINDOW)], own_sem.at[0]
+            k_hbm.at[:, cols_of(me)], kv.at[0, rows_of(tok * n_head + me, rd)], own_sem.at[0]
         ),
         pltpu.make_async_copy(
-            v_hbm.at[:, cols_of(me)], vw.at[rows_of(me, rd, WINDOW)], own_sem.at[1]
+            v_hbm.at[:, cols_of(me)], kv.at[1, rows_of(tok * n_head + me, rd)], own_sem.at[1]
         ),
         pltpu.make_async_copy(q_hbm.at[:, cols_of(me)], qw.at[rows_of(me, rd)], own_sem.at[2]),
     )
@@ -134,36 +134,40 @@
     def _(step):
         q_copy(me, lax.rem(me + step, n_head)).start()
 
+    def r_copy(source, target):
+        return pltpu.make_async_remote_copy(
+            src_ref=rate_ref,
+            dst_ref=rates.at[source],
+            send_sem=r_send.at[target],
+            recv_sem=r_recv.at[source],
+            device_id=(target, me),
+            device_id_type=MESH,
+        )
+
+    @pl.loop(1, n_tok)
+    def _(step):
+        r_copy(tok, lax.rem(tok + step, n_tok)).start()
+
     acc[...] = jnp.zeros_like(acc)
-
-    @pl.when(tok == 0)
-    def _():
-        kw[0:WINDOW, :] = jnp.zeros((WINDOW, DH), jnp.bfloat16)
-        vw[0:WINDOW, :] = jnp.zeros((WINDOW, DH), jnp.bfloat16)
-
-    @pl.loop(0, rs.shape[0] // 128)
-    def _(index):
-        part = rate_ref[:, rows_of(index, 128)]
-        rs[rows_of(index, 128), :] = -jnp.broadcast_to(part, (128, 128)).T
+    rates[tok] = rate_ref[...]
 
     for copy in own_copies:
         copy.wait()
 
-    def halo_copy(local, halo, send, recv, part):
+    def f_copy(source, target, group):
+        rows = rows_of(source * groups + group, rg)
         return pltpu.make_async_remote_copy(
-            src_ref=local.at[rows_of(part + groups, rg)],
-            dst_ref=halo.at[rows_of(part, rg)],
-            send_sem=send.at[part],
-            recv_sem=recv.at[part],
-            device_id=(jnp.minimum(tok + 1, n_tok - 1), me),
+            src_ref=kv.at[:, rows],
+            dst_ref=kv.at[:, rows],
+            send_sem=f_send.at[target, group],
+            recv_sem=f_recv.at[source, group],
+            device_id=(target, me),
             device_id_type=MESH,
         )
 
-    def hk_copy(part):
-        return halo_copy(kw, kw, hk_send, hk_recv, part)
-
-    def hv_copy(part):
-        return halo_copy(vw, vw, hv_send, hv_recv, part)
+    @pl.loop(1, n_tok)
+    def _(step):
+        r_copy(lax.rem(tok + step, n_tok), tok).wait_recv()
 
     def group_at(step):
         return lax.rem(mine - step + groups, groups)
@@ -177,22 +181,13 @@
                 for copy in copies:
                     copy(source, me).wait_recv()
 
-    @pl.loop(0, groups)
-    def _(step):
-        group = group_at(step)
-        wait_group(group, (k_copy, v_copy))
-        part = group - (groups - halo_groups)
-
-        @pl.when(jnp.logical_and(part >= 0, tok < n_tok - 1))
-        def _():
-            hk_copy(part).start()
-            hv_copy(part).start()
-
-        keys = kw[rows_of(group, rg, WINDOW), :]
-        values = vw[rows_of(group, rg, WINDOW), :].astype(jnp.float32)
-        rates = rs[rows_of(group, rg), :]
+    def contribute(source, group):
+        rows = rows_of(source * groups + group, rg)
+        keys = kv[0, rows, :]
+        values = kv[1, rows, :].astype(jnp.float32)
+        rate = -jnp.broadcast_to(rates[source, :, rows_of(group, rg)], (128, rg)).T
         target = jnp.concatenate(
-            [values[:, :128] * rates, values[:, 128:] * rates], axis=1
+            [values[:, :128] * rate, values[:, 128:] * rate], axis=1
         )
         target = target.astype(jnp.bfloat16)
         gate = dot_nt(keys, w_ref[0, :, 0:DH])
@@ -209,44 +204,48 @@
         acc[1] += dot_nn(keys_t, up_grad)
         acc[2] += dot_nn(turned(target), hidden)
 
-    def g_copy(source, target):
-        return pltpu.make_async_remote_copy(
-            src_ref=grads.at[source],
-            dst_ref=grads.at[source],
-            send_sem=g_send.at[target],
-            recv_sem=g_recv.at[source],
-            device_id=(target, me),
-            device_id_type=MESH,
-        )
-
-    grads[tok] = acc[...].astype(jnp.bfloat16)
-
-    @pl.loop(1, n_tok)
-    def _(step):
-        g_copy(tok, lax.rem(tok + step, n_tok)).start()
-
-    @pl.when(tok > 0)
-    def _():
-        @pl.loop(0, halo_groups)
-        def _(part):
-            hk_copy(part).wait_recv()
-            hv_copy(part).wait_recv()
+    @pl.loop(0, groups + 1)
+    def _(step):
+        @pl.loop(0, n_tok)
+        def _(hop):
+            source = lax.rem(tok + hop, n_tok)
+            own = hop == 0
+            group = group_at(jnp.where(own, step, step - 1))
+
+            @pl.when(jnp.logical_and(own, step < groups))
+            def _():
+                wait_group(group, (k_copy, v_copy))
+
+                @pl.loop(1, n_tok)
+                def _(other):
+                    f_copy(tok, lax.rem(tok + other, n_tok), group).start()
+
+            @pl.when(jnp.logical_and(hop > 0, step > 0))
+            def _():
+                f_copy(source, tok, group).wait_recv()
+
+            @pl.when(jnp.where(own, step < groups, step > 0))
+            def _():
+                contribute(source, group)
 
     row = lax.broadcasted_iota(jnp.int32, (rg, rg), 0)
     col = lax.broadcasted_iota(jnp.int32, (rg, rg), 1)
+
+    def seen_chunk(group, chunk):
+        return jnp.maximum(first + group + chunk - halo_groups, 0)
 
     def attend(group):
         wait_group(group, (q_copy,))
         queries = qw[rows_of(group, rg), :]
         scores = []
         for chunk in range(halo_groups + 1):
-            value = dot_nt(queries, kw[rows_of(group + chunk, rg), :])
+            value = dot_nt(queries, kv[0, rows_of(seen_chunk(group, chunk), rg), :])
             if chunk == 0:
                 value = jnp.where(col > row, value, MASKED)
             if chunk == halo_groups:
                 value = jnp.where(col <= row, value, MASKED)
             else:
-                seen = jnp.logical_or(tok > 0, group + chunk >= halo_groups)
+                seen = first + group + chunk >= halo_groups
                 value = value + jnp.where(seen, 0.0, MASKED)
             scores.append(value)
         highest = functools.reduce(jnp.maximum, scores)
@@ -257,23 +256,13 @@
             expo = jnp.exp2((scores[chunk] - highest) * (LOG2E * DH ** (-0.5)))
             total = total + expo
             result = result + dot_nn(
-                expo.astype(jnp.bfloat16), vw[rows_of(group + chunk, rg), :]
+                expo.astype(jnp.bfloat16), kv[1, rows_of(seen_chunk(group, chunk), rg), :]
             )
         result = result / jnp.sum(total, axis=1, keepdims=True)
-        att[rows_of(group, rg), :] = rms_norm(result)
-
-    @pl.loop(0, early)
-    def _(step):
-        attend(group_at(step))
-
-    @pl.loop(1, n_tok)
-    def _(step):
-        g_copy(lax.rem(tok + step, n_tok), tok).wait_recv()
+        return rms_norm(result)
 
     for block in range(3):
-        total = grads[0, block].astype(jnp.float32)
-        for index in range(1, n_tok):
-            total = total + grads[index, block].astype(jnp.float32)
+        total = acc[block]
         squares = jnp.sum(
             jnp.sum(total * total, axis=1, keepdims=True), axis=0, keepdims=True
         )
@@ -301,20 +290,16 @@
             w_ref[0, :, columns].astype(jnp.float32) - zs[block].astype(jnp.float32).T
         ).astype(jnp.bfloat16)
 
-    @pl.loop(1, groups + 1)
+    @pl.loop(0, groups)
     def _(step):
         group = group_at(step)
-
-        @pl.when(jnp.logical_and(step >= early, step < groups))
-        def _():
-            attend(group)
-
+        attended = attend(group)
         queries = qw[rows_of(group, rg), :]
         gate = dot_nt(queries, wnew[:, 0:DH])
         up = dot_nt(queries, wnew[:, DH : 2 * DH])
         hidden = (gate * sigmoid(gate) * up).astype(jnp.bfloat16)
         applied = rms_norm(dot_nn(hidden, wnew[:, 2 * DH :]))
-        obuf[rows_of(group, rg), :] = (att[rows_of(group, rg), :] + applied).astype(
+        obuf[rows_of(group, rg), :] = (attended + applied).astype(
             jnp.bfloat16
         )
         for core in range(2):
@@ -341,14 +326,12 @@
 
     @pl.loop(1, n_tok)
     def _(step):
-        g_copy(tok, lax.rem(tok + step, n_tok)).wait_send()
-
-    @pl.when(tok < n_tok - 1)
-    def _():
-        @pl.loop(0, halo_groups)
-        def _(part):
-            hk_copy(part).wait_send()
-            hv_copy(part).wait_send()
+        target = lax.rem(tok + step, n_tok)
+        r_copy(tok, target).wait_send()
+
+        @pl.loop(0, groups)
+        def _(group):
+            f_copy(tok, target, group).wait_send()
 
     @pl.loop(1, n_head)
     def _(step):
@@ -362,7 +345,7 @@
     n_head = lax.axis_size("head")
     rd, width = query_states.shape
     rows = rd * n_head
-    halo_groups = WINDOW // (2 * rd)
+    groups = n_head // 2
     dma = pltpu.SemaphoreType.DMA
     heads_sems = [dma((n_head,))] * 8
     return pl.pallas_call(
@@ -378,22 +361,17 @@
             pl.BlockSpec(memory_space=pltpu.VMEM),
         ),
         scratch_shapes=[
-            pltpu.VMEM((WINDOW + rows, DH), jnp.bfloat16),
-            pltpu.VMEM((WINDOW + rows, DH), jnp.bfloat16),
+            pltpu.VMEM((2, n_tok * rows, DH), jnp.bfloat16),
             pltpu.VMEM((rows, DH), jnp.bfloat16),
-            pltpu.VMEM((rows, 128), jnp.float32),
-            pltpu.VMEM((rows, DH), jnp.float32),
+            pltpu.VMEM((n_tok, 1, rows), jnp.float32),
             pltpu.VMEM((3, DH, FH), jnp.float32),
-            pltpu.VMEM((n_tok, 3, DH, FH), jnp.bfloat16),
             pltpu.VMEM((3, DH, FH), jnp.bfloat16),
             pltpu.VMEM((FH, 3 * DH), jnp.bfloat16),
             pltpu.VMEM((rows, DH), jnp.bfloat16),
             dma((4,)),
             *heads_sems,
-            dma((halo_groups,)),
-            dma((halo_groups,)),
-            dma((halo_groups,)),
-            dma((halo_groups,)),
+            dma((n_tok, groups)),
+            dma((n_tok, groups)),
             dma((n_tok,)),
             dma((n_tok,)),
         ],

time: 117 us -> 122 us (1.043)
  Pallas kernels: 113 us -> 118 us
    pallas_call x1, Pallas kernels: 113 us -> 118 us  [per_device(): pl.pallas_call(functools.partial(layer_kernel, n_tok, n_head), out_shape=...]
where the time goes in v2:
time: 122 us
  Pallas kernels  118 us (97%)
  local copies, waits for them, and re-layouts  3.09 us (3%)
    pallas_call x1, Pallas kernels, per_device(): pl.pallas_call(functools.partial(layer_kernel, n_tok, n_head), out_shape=...  118 us
    unnamed x4, local copies, waits for them, and re-layouts  3.09 us

profile of v2, /device:TPU:1, one launch (start us, length us, event | category | flops | bytes accessed | tf_op | source)
XLA Modules:
  0.0 122.0 jit_solution(439766322410426381)
XLA Ops:
  0.6 118.3 %layer.1 = (bf16[128,4096]{1,0:T(8,128)(2,1)}, bf16[1,256,768]{2,1,0:T(8,128)(2,1)}) custom-call(bf16[128,4096]{1,0:T(8,128)(2,1)} %q_hbm.1, bf16[128,4096]{1,0:T(8,128)(2,1)} %k_hbm.1, bf16[128,4096]{1,0:T(8,128)(2,1)} %v_hbm.1, f32[1,2048]{1,0:T(1,128)} %rate_ref.1, bf16[1,512,768]{2,1,0:T(8,128)(2,1)} %w_ref.1), custom_call_target="tpu_custom_call" | custom-call | tf_op jit(solution)/shard_map/layer/pallas_call | solution.py:351
  118.9 0.0 copy-start
  118.9 2.3 %copy.9 = bf16[128,4096]{1,0:T(8,128)(2,1)} copy(bf16[128,4096]{1,0:T(8,128)(2,1)} %get-tuple-element.4) | data formatting | bytes 2097152
  121.3 0.0 copy-done
  121.3 0.7 copy.10
Async XLA Ops:
  118.9 2.4 %copy-start = (bf16[1,256,768]{2,1,0:T(8,128)(2,1)S(1)}, bf16[1,256,768]{2,1,0:T(8,128)(2,1)}, u32[]{:S(2)}) copy-start(bf16[1,256,768]{2,1,0:T(8,128)(2,1)} %get-tuple-element.5) | copy-start | bytes 1179652

commit v3 on v2

--- a/solution.py
+++ b/solution.py
@@ -60,6 +60,8 @@
     halo_groups = WINDOW // rg
     mine = lax.div(me, 2)
     first = tok * groups
+    stride = 3 if groups % 3 else 1
+    window = min(3, groups)
 
     barrier = pltpu.get_barrier_semaphore()
 
@@ -124,15 +126,18 @@
 
     pl.semaphore_wait(barrier, n_head - 1 + n_tok - 1)
 
-    @pl.loop(1, n_head)
-    def _(step):
-        target = lax.rem(me + step, n_head)
-        k_copy(me, target).start()
-        v_copy(me, target).start()
-
-    @pl.loop(1, n_head)
-    def _(step):
-        q_copy(me, lax.rem(me + step, n_head)).start()
+    def send(step, copies):
+        for core in range(2):
+            target = lax.rem(mine + stride * step, groups) * 2 + core
+
+            @pl.when(target != me)
+            def _():
+                for copy in copies:
+                    copy(me, target).start()
+
+    @pl.loop(0, window)
+    def _(step):
+        send(step, (k_copy, v_copy))
 
     def r_copy(source, target):
         return pltpu.make_async_remote_copy(
@@ -170,7 +175,7 @@
         r_copy(lax.rem(tok + step, n_tok), tok).wait_recv()
 
     def group_at(step):
-        return lax.rem(mine - step + groups, groups)
+        return lax.rem(mine + stride * (groups - step), groups)
 
     def wait_group(group, copies):
         for core in range(2):
@@ -210,7 +215,7 @@
         def _(hop):
             source = lax.rem(tok + hop, n_tok)
             own = hop == 0
-            group = group_at(jnp.where(own, step, step - 1))
+            group = group_at(jnp.where(own, step, jnp.maximum(step - 1, 0)))
 
             @pl.when(jnp.logical_and(own, step < groups))
             def _():
@@ -219,6 +224,16 @@
                 @pl.loop(1, n_tok)
                 def _(other):
                     f_copy(tok, lax.rem(tok + other, n_tok), group).start()
+
+                @pl.when(step + window < groups)
+                def _():
+                    send(step + window, (k_copy, v_copy))
+
+                @pl.when(step == groups - window)
+                def _():
+                    @pl.loop(0, groups)
+                    def _(later):
+                        send(later, (q_copy,))
 
             @pl.when(jnp.logical_and(hop > 0, step > 0))
             def _():

time: 122 us -> 108 us (0.89); the launches traced: 122 us -> 106 us
  Pallas kernels: 118 us -> 102 us
    pallas_call x1, Pallas kernels: 118 us -> 102 us  [per_device(): pl.pallas_call(functools.partial(layer_kernel, n_tok, n_head), out_shape=...]
where the time goes in v3:
time: 108 us; the launch traced here: 106 us
  Pallas kernels  102 us (94%)
  local copies, waits for them, and re-layouts  3.09 us (3%)
    pallas_call x1, Pallas kernels, per_device(): pl.pallas_call(functools.partial(layer_kernel, n_tok, n_head), out_shape=...  102 us
    unnamed x4, local copies, waits for them, and re-layouts  3.09 us

profile of v3, /device:TPU:1, one launch (start us, length us, event | category | flops | bytes accessed | tf_op | source)
XLA Modules:
  0.0 106.0 jit_solution(533100244241087112)
XLA Ops:
  0.6 102.2 %layer.1 = (bf16[128,4096]{1,0:T(8,128)(2,1)}, bf16[1,256,768]{2,1,0:T(8,128)(2,1)}) custom-call(bf16[128,4096]{1,0:T(8,128)(2,1)} %q_hbm.1, bf16[128,4096]{1,0:T(8,128)(2,1)} %k_hbm.1, bf16[128,4096]{1,0:T(8,128)(2,1)} %v_hbm.1, f32[1,2048]{1,0:T(1,128)} %rate_ref.1, bf16[1,512,768]{2,1,0:T(8,128)(2,1)} %w_ref.1), custom_call_target="tpu_custom_call" | custom-call | tf_op jit(solution)/shard_map/layer/pallas_call | solution.py:366
  102.9 0.0 copy-start
  102.9 2.3 %copy.9 = bf16[128,4096]{1,0:T(8,128)(2,1)} copy(bf16[128,4096]{1,0:T(8,128)(2,1)} %get-tuple-element.4) | data formatting | bytes 2097152
  105.2 0.0 copy-done
  105.2 0.7 copy.10
Async XLA Ops:
  102.9 2.4 %copy-start = (bf16[1,256,768]{2,1,0:T(8,128)(2,1)S(1)}, bf16[1,256,768]{2,1,0:T(8,128)(2,1)}, u32[]{:S(2)}) copy-start(bf16[1,256,768]{2,1,0:T(8,128)(2,1)} %get-tuple-element.5) | copy-start | bytes 1179652
